TPU v7x, 32 devices: a whole 2x2x4 slice. The times are simulated.
32 devices in a mesh: energy: 4 (over z), views: 8 (over y, x, core).
Axes of the slice: x: 2, y: 2, z: 4, core: 2. Of those that a mesh axis runs over, the one named last changes fastest.
Arguments:
- projector_tiles: float32 [32, 48, 128, 256], P('views'), may hold values from -0.0546875 to 0.0546875
- tile_blocks: int32 [32, 48], P('views'), may hold values from 0 to 63
- ray_counts: int32 [32], P('views'), may hold values from 64 to 128
- sinogram: float32 [64, 4096], P('energy', 'views'), may hold values from -6 to 6
- ray_weights: float32 [64, 4096], P('energy', 'views'), may hold values from 0.25 to 4
- start_volume: float32 [64, 16384], P('energy', 'views'), may hold values from -6 to 6
- split_target: float32 [8, 64, 2048], P('views', None, 'energy'), may hold values from -6 to 6
- scaled_dual: float32 [8, 64, 2048], P('views', None, 'energy'), may hold values from -3 to 3
Outputs:
- new_volume: float32 [64, 16384], P('energy', 'views')
- new_split: float32 [8, 64, 2048], P('views', None, 'energy')
- new_dual: float32 [8, 64, 2048], P('views', None, 'energy')
Inputs may be any that keep to these rules, and one draw needn't show every extreme that they name: `tile_blocks`: block indices may repeat within a ray block. `ray_counts`: rays of a block at or past its count are padding.
All inputs are finite; a program needn't handle non-finite values.
Results may differ from a plain program's by a relative error of at most 0.00022.
Values sent between devices are 32-bit elements; how exact they have to be, the bound alone decides.
No kernel may reach another device: no remote copies, remote signals or barrier semaphores. Data moves between devices by JAX's collectives and lax.ppermute only.
A program may use at most 128 MiB of HBM per device.

v0:
```python
import functools

import jax
import jax.numpy as jnp
from jax import lax
from jax.experimental import pallas as pl
from jax.experimental.pallas import tpu as pltpu
from jax.sharding import PartitionSpec as P

PV = 64
ITERS = 3
PENALTY = 1.0
SHRINK = 16.0
LANES = 128
LOOPED = ("first", "mid")
PIVOTS = 2
F32, BF16 = jnp.float32, jnp.bfloat16

VM = pl.BlockSpec(memory_space=pltpu.VMEM)
SM = pl.BlockSpec(memory_space=pltpu.SMEM)
ANY = pl.BlockSpec(memory_space=pl.ANY)
MIB = 1 << 20


def sds(shape, dtype=F32):
    return jax.ShapeDtypeStruct(shape, dtype)


def call(body, outs, ins, specs, scratch=(), limit=12, flops=0, moved=0, out_specs=None, name=None):
    return pl.pallas_call(
        body,
        out_shape=outs,
        in_specs=specs,
        out_specs=out_specs if out_specs is not None else jax.tree.map(lambda _: VM, outs),
        scratch_shapes=list(scratch),
        compiler_params=pltpu.CompilerParams(vmem_limit_bytes=limit * MIB),
        cost_estimate=pl.CostEstimate(flops=flops, bytes_accessed=moved, transcendentals=0),
        name=name,
    )(*ins)


def halves(x):
    hi = x.astype(BF16).astype(F32)
    return hi, x - hi


def prepare(tiles, ids, step, depth=6):
    R, T, rays, width = tiles.shape
    per = T // step
    trips = R * per

    def body(ids_ref, src, out, token, buf, sem):
        token[...] = jnp.zeros_like(token)

        def copy(i):
            slot = lax.rem(i, depth)
            at = lax.rem(i, per) * step
            return pltpu.make_async_copy(src.at[i // per, pl.ds(at, step)], buf.at[slot], sem.at[slot])

        for a in range(depth - 1):
            copy(a).start()

        def trip(i, carry):
            @pl.when(i + depth - 1 < trips)
            def _():
                copy(i + depth - 1).start()

            copy(i).wait()
            slot = lax.rem(i, depth)
            r, base = i // per, lax.rem(i, per) * step
            for a in range(step):
                hi, lo = halves(buf[slot, a])
                at = pl.multiple_of((base + a) * width, width)
                out[r, :rays, pl.ds(at, width)] = hi.astype(BF16)
                out[r, rays:, pl.ds(at, width)] = lo.astype(BF16)
            return carry

        lax.fori_loop(0, trips, trip, 0)

    return call(
        body,
        [pltpu.VMEM((R, 2 * rays, T * width), BF16), sds((8, LANES))],
        (ids, tiles),
        [SM, ANY],
        [pltpu.VMEM((depth, step, rays, width), F32), pltpu.SemaphoreType.DMA((depth,))],
        moved=tiles.size * 8,
        flops=tiles.size * 4,
        name="prepare",
    )


def apply_body(mode, dims, refs):
    n, C, seg, R, T, rays, vb = dims
    nb = seg // vb
    ext = LANES if mode != "first" else 0
    it = iter(refs)
    me_ref, blocks = next(it), next(it)
    pieces = [next(it) for _ in range(n)]
    tt, scale_ref = next(it), next(it)
    if mode == "first":
        sino, _ = next(it), next(it)
    if mode in ("mid", "last"):
        d_prev, ad_prev, rr_prev = next(it), next(it), next(it)
    if mode != "last":
        keep = [next(it) for _ in range(n // 2)]
        send = [next(it) for _ in range(n // 2)]
    if mode == "last":
        scal_out = next(it)
    if mode != "first":
        d_out, rr_out = next(it), next(it)
    if mode in ("zero", "mid"):
        ad_out = next(it)
    vs = next(it)
    weighted = next(it)
    columns = next(it)
    acc = next(it) if mode != "last" else None
    me = me_ref[0]

    for i in range(n):
        dev = me ^ i
        for j in range(nb):
            hi, lo = halves(pieces[i][:, j * vb : (j + 1) * vb])
            vs[dev * nb + j] = jnp.concatenate([hi, lo], axis=0).astype(BF16)

    partial = jnp.zeros((C, LANES), F32)
    beta = None
    if mode != "first":
        parts = pieces[0][:, seg:]
        for i in range(1, n):
            parts = parts + pieces[i][:, seg:]
        rr = jnp.sum(parts, axis=1, keepdims=True)
        rr_out[...] = jnp.broadcast_to(rr, (C, LANES))
        d = pieces[0][:, :seg]
        if mode != "zero":
            beta = rr / rr_prev[:, :1]
            d = d + beta * d_prev[...]
        d_out[...] = d
        squares = d * d
        for j in range(seg // LANES):
            partial = partial + squares[:, j * LANES : (j + 1) * LANES]

    for r in range(R):
        for t in range(T):
            columns[:, t * vb : (t + 1) * vb] = vs[blocks[r, t]]
        total = lax.dot_general(
            tt[r], columns[...], (((1,), (1,)), ((), ())), preferred_element_type=F32
        ).T
        both = total[:C] + total[C:]
        ray = both[:, :rays] + both[:, rays:]
        here = slice(r * rays, (r + 1) * rays)
        scale = scale_ref[:, here]
        if mode == "first":
            weight = scale * (sino[:, here] - ray)
        else:
            if mode != "zero":
                ray = ray + beta * ad_prev[:, here]
            if mode != "last":
                ad_out[:, here] = ray
            weight = scale * ray
            product = weight * ray
            for j in range(rays // LANES):
                partial = partial + product[:, j * LANES : (j + 1) * LANES]
        if mode != "last":
            hi, lo = halves(weight)
            stacked = jnp.concatenate([hi, lo], axis=0)
            weighted[r] = jnp.concatenate([stacked, stacked], axis=1).astype(BF16)
    if mode == "last":
        scal_out[...] = partial
        return

    acc[...] = jnp.zeros_like(acc)
    def back(r, carry):
        lhs = weighted[r]

        for t in range(T):
            out = lax.dot_general(
                lhs, tt[r, :, t * vb : (t + 1) * vb], (((1,), (0,)), ((), ())), preferred_element_type=F32
            )
            b = blocks[r, t]
            acc[b] = acc[b] + (out[:C] + out[C:])
        return carry

    if mode in LOOPED:
        lax.fori_loop(0, R, back, 0)
    else:
        for r in range(R):
            back(r, 0)

    for j in range(n // 2):
        for dest, out in ((me ^ (2 * j), keep[j]), (me ^ (2 * j + 1), send[j])):
            for q in range(nb):
                out[:, q * vb : (q + 1) * vb] = acc[dest * nb + q]
            if ext:
                out[:, seg:] = partial


def apply(mode, dims, *ins):
    n, C, seg, R, T, rays, vb = dims
    ext = LANES if mode != "first" else 0
    outs = []
    if mode != "last":
        outs += [sds((C, seg + ext))] * n
    else:
        outs += [sds((C, LANES))]
    if mode != "first":
        outs += [sds((C, seg)), sds((C, LANES))]
    if mode in ("zero", "mid"):
        outs += [sds((C, R * rays))]
    scratch = [
        pltpu.VMEM((n * (seg // vb), 2 * C, vb), BF16),
        pltpu.VMEM((R, 2 * C, 2 * rays), BF16),
        pltpu.VMEM((2 * C, T * vb), BF16),
    ]
    if mode != "last":
        scratch.append(pltpu.VMEM((n * (seg // vb), C, vb), F32))
    specs = [SM, SM] + [VM] * (len(ins) - 2)
    return call(
        lambda *refs: apply_body(mode, dims, refs),
        outs,
        ins,
        specs,
        scratch,
        flops=4 * C * R * T * rays * vb,
        moved=R * T * rays * vb * 4,
        name="apply_" + mode,
    )


def fold(x):
    total = x[:, :LANES]
    for j in range(1, x.shape[1] // LANES):
        total = total + x[:, j * LANES : (j + 1) * LANES]
    return total


def update_first(parts, volume, target):
    C, seg = volume.shape

    def body(*refs):
        got = refs[: len(parts)]
        vol, tgt, out = refs[len(parts) :]
        total = got[0][...]
        for g in got[1:]:
            total = total + g[...]
        r = total + PENALTY * (tgt[...] - vol[...])
        out[:, :seg] = r
        out[:, seg:] = fold(r * r)

    return call(body, sds((C, seg + LANES)), (*parts, volume, target), [VM] * (len(parts) + 2), name="update_first")


def update(parts, volume, residual, direction, rr):
    C, seg = volume.shape

    def body(*refs):
        got = refs[: len(parts)]
        vol, res, dirn, rr_ref, vol_out, out = refs[len(parts) :]
        total = got[0][...]
        for g in got[1:]:
            total = total + g[...]
        d = dirn[...]
        alpha = rr_ref[:, :1] / jnp.sum(total[:, seg:], axis=1, keepdims=True)
        vol_out[...] = vol[...] + alpha * d
        r = res[:, :seg] - alpha * (total[:, :seg] + PENALTY * d)
        out[:, :seg] = r
        out[:, seg:] = fold(r * r)

    return call(
        body,
        [sds((C, seg)), sds((C, seg + LANES))],
        (*parts, volume, residual, direction, rr),
        [VM] * (len(parts) + 4),
        name="update",
    )


def finish(parts, volume, direction, rr, group, E):
    C, seg = volume.shape
    width = seg // E

    def body(*refs):
        e_ref, got = refs[0], refs[1 : 1 + len(parts)]
        vol, dirn, rr_ref, vol_out = refs[1 + len(parts) : 5 + len(parts)]
        outs = refs[5 + len(parts) :]
        total = got[0][...]
        for g in got[1:]:
            total = total + g[...]
        alpha = rr_ref[:, :1] / jnp.sum(total, axis=1, keepdims=True)
        vol_out[...] = vol[...] + alpha * dirn[...]
        for k in range(E):
            at = pl.multiple_of((e_ref[1] ^ k) * width, LANES)
            outs[k][...] = vol_out[:, pl.ds(at, width)]

    got = call(
        body,
        [sds((C, seg))] + [sds((C, width))] * E,
        (group, *parts, volume, direction, rr),
        [SM] + [VM] * (len(parts) + 3),
        name="finish",
    )
    return got[0], got[1:]


def split_target_pieces(split_target, scaled_dual, group, E):
    full, width = split_target.shape
    C = full // E

    def body(e_ref, st, sd, *outs):
        for k in range(E):
            at = pl.multiple_of((e_ref[1] ^ k) * C, 8)
            outs[k][...] = st[pl.ds(at, C), :] - sd[pl.ds(at, C), :]

    return call(body, [sds((C, width))] * E, (group, split_target, scaled_dual), [SM, VM, VM], name="target_pieces")


def join_target(pieces, group):
    E = len(pieces)
    C, width = pieces[0].shape

    def body(e_ref, *refs):
        for k in range(E):
            at = pl.multiple_of((e_ref[1] ^ k) * width, LANES)
            refs[E][:, pl.ds(at, width)] = refs[k][...]

    return call(body, sds((C, width * E)), (group, *pieces), [SM] + [VM] * E, name="join_target")


def shrink(pieces, scaled_dual, group):
    E = len(pieces)
    C, width = pieces[0].shape
    N = C * E
    patches = width // PV

    def body(e_ref, *refs):
        got, sd = refs[:E], refs[E]
        split_out, dual_out, vol, aug, rows, solved = refs[E + 1 :]
        for k in range(E):
            at = pl.multiple_of((e_ref[1] ^ k) * C, 8)
            vol[pl.ds(at, C), :] = got[k][...]
        lane = lax.broadcasted_iota(jnp.int32, (N, 2 * PV), 1)
        left = lane < PV
        diag = jnp.where(lane == lax.broadcasted_iota(jnp.int32, (N, 2 * PV), 0), F32(SHRINK), F32(0))
        for q in range(patches // 2):
            here = slice(q * 2 * PV, (q + 1) * 2 * PV)
            pair = vol[:, here] + sd[:, here]
            turned = pltpu.roll(pair, PV, 1)
            for h, (first, other) in enumerate(((pair, turned), (turned, pair))):
                only = jnp.where(left, first, 0.0)
                gram = lax.dot_general(
                    only, jnp.concatenate([first, first], axis=0), (((1,), (1,)), ((), ())),
                    precision=lax.Precision.HIGHEST, preferred_element_type=F32,
                )
                p = 2 * q + h
                aug[p * N : (p + 1) * N, :] = jnp.where(left, gram + diag, other)
        lane8 = lax.broadcasted_iota(jnp.int32, (patches, 2 * PV), 1)
        for i in range(N):
            rows[i] = aug[pl.ds(i, patches, stride=N), :]
        for k in range(0, N, PIVOTS):
            span = range(PIVOTS)
            top = [rows[k + q] for q in span]
            small = [[jnp.broadcast_to(top[q][:, k + s : k + s + 1], top[q].shape) for s in span] for q in span]
            for q in span:
                inverse = 1.0 / small[q][q]
                top[q] = top[q] * inverse
                small[q] = [x * inverse for x in small[q]]
                for s in span:
                    if s != q:
                        factor = small[s][q]
                        top[s] = top[s] - factor * top[q]
                        small[s] = [x - factor * y for x, y in zip(small[s], small[q])]
            top = [jnp.where(lane8 >= k, x, 0.0) for x in top]
            for q in span:
                rows[k + q] = top[q]
            for i in list(range(k + PIVOTS, N)) + list(range(k)):
                other = rows[i]
                new = other
                for q in span:
                    new = new - other[:, k + q : k + q + 1] * top[q]
                rows[i] = new
        for i in range(N):
            solved[pl.ds(i, patches, stride=N), :] = rows[i]
        for q in range(patches // 2):
            here = slice(q * 2 * PV, (q + 1) * 2 * PV)
            even = solved[2 * q * N : (2 * q + 1) * N, :]
            odd = solved[(2 * q + 1) * N : (2 * q + 2) * N, :]
            both = jnp.where(left, pltpu.roll(even, PV, 1), odd)
            patch, dual = vol[:, here], sd[:, here]
            result = (patch + dual) - SHRINK * both
            split_out[:, here] = result
            dual_out[:, here] = dual + patch - result

    return call(
        body,
        [sds((N, width))] * 2,
        (group, *pieces, scaled_dual),
        [SM] + [VM] * (E + 1),
        [
            pltpu.VMEM((N, width), F32),
            pltpu.VMEM((patches * N, 2 * PV), F32),
            pltpu.VMEM((N, patches, 2 * PV), F32),
            pltpu.VMEM((patches * N, 2 * PV), F32),
        ],
        name="shrink",
    )


def swap(x, axis, size, k):
    return lax.ppermute(x, axis, [(i, i ^ k) for i in range(size)])


def gather(own, n, between=None):
    pieces = [None] * n
    pieces[0] = own
    for j in range(n // 2 - 1, 0, -1):
        pieces[2 * j] = swap(own, "views", n, 2 * j)
    if between is not None:
        pieces[2::2] = [piece + between for piece in pieces[2::2]]
    for j in range(n // 2):
        pieces[2 * j + 1] = swap(pieces[2 * j], "views", n, 1)
    return pieces


def scatter_sum(keep, send, n):
    got = [None] * (n // 2)
    for j in range(n // 2 - 1, -1, -1):
        got[j] = swap(send[j], "views", n, 1)
    parts = [keep[0], got[0]]
    for j in range(n // 2 - 1, 0, -1):
        parts.append(swap(keep[j] + got[j], "views", n, 2 * j))
    return parts


def local(tiles, tile_blocks, ray_counts, sinogram, ray_weights, start, split_target, scaled_dual):
    n, E = lax.axis_size("views"), lax.axis_size("energy")
    C, seg = start.shape
    R, T, rays, vb = tiles.shape
    dims = (n, C, seg, R, T, rays, vb)
    me = group = jnp.stack([lax.axis_index("views"), lax.axis_index("energy")]).astype(jnp.int32)
    live = (lax.broadcasted_iota(jnp.int32, (R, rays), 1) < ray_counts[:, None]).astype(F32)
    scale = ray_weights * live.reshape(1, -1)
    split_target, scaled_dual = split_target[0], scaled_dual[0]

    tt, token = prepare(tiles, me, 8)
    tp = split_target_pieces(split_target, scaled_dual, group, E)
    pieces = gather(start, n, token[0, 0])
    tp = [tp[0]] + [swap(tp[k], "energy", E, k) for k in range(1, E)]
    target = join_target(tp, group)

    out = apply("first", dims, me, tile_blocks, *pieces, tt, scale, sinogram, target)
    parts = scatter_sum(out[: n // 2], out[n // 2 : n], n)
    residual = update_first(parts, start, target)
    volume = start

    d = ad = rr = None
    for it in range(ITERS):
        pieces = gather(residual, n)
        mode = "zero" if it == 0 else ("mid" if it + 1 < ITERS else "last")
        ins = (me, tile_blocks, *pieces, tt, scale)
        if it:
            ins += (d, ad, rr)
        out = apply(mode, dims, *ins)
        if mode == "last":
            scal, d, rr = out
            break
        d, rr, ad = out[n:]
        parts = scatter_sum(out[: n // 2], out[n // 2 : n], n)
        volume, residual = update(parts, volume, residual, d, rr)

    scal = scal + swap(scal, "views", n, 1)
    parts = [scal] + [swap(scal, "views", n, 2 * j) for j in range(n // 2 - 1, 0, -1)]
    volume, vp = finish(parts, volume, d, rr, group, E)
    vp = [vp[0]] + [swap(vp[k], "energy", E, k) for k in range(1, E)]
    new_split, new_dual = shrink(vp, scaled_dual, group)
    return volume, new_split[None], new_dual[None]


def solution(mesh):
    placed = (
        P("views", None, None, None),
        P("views", None),
        P("views"),
        P("energy", "views"),
        P("energy", "views"),
        P("energy", "views"),
        P("views", None, "energy"),
        P("views", None, "energy"),
    )
    return jax.shard_map(
        local,
        mesh=mesh,
        in_specs=placed,
        out_specs=(P("energy", "views"), P("views", None, "energy"), P("views", None, "energy")),
        check_vma=False,
    )
```

profile of v0, /device:TPU:0, one launch (start us, length us, event | category | flops | bytes accessed | tf_op | source)
XLA Modules:
  0.0 165.2 jit_solution(11080401019436844432)
XLA Ops:
  0.6 4.0 %collective-permute-start.5 = (f32[16,2048]{1,0:T(8,128)}, f32[16,2048]{1,0:T(8,128)S(1)}, u32[]{:S(2)}, u32[]{:S(2)}) collective-permute-start(f32[16,2048]{1,0:T(8,128)} %refs_5_.3), channel_id=1, source_target_pairs={{0,6},{1,7},{2,4},{3,5},{4,2},{5,3},{6,0},{7,1},{8,14},{9,15},{10,... | collective-permute-start | bytes 393224 | tf_op jit(solution)/shard_map/ppermute | solution.py:408
  7.7 2.0 %collective-permute-start.7 = (f32[16,512]{1,0:T(8,128)S(1)}, f32[16,512]{1,0:T(8,128)S(1)}, u32[]{:S(2)}, u32[]{:S(2)}) collective-permute-start(f32[16,512]{1,0:T(8,128)S(1)} %get-tuple-element.56), channel_id=1, source_target_pairs={{0,8},{8,0},{16,24},{24,16},{1,9},{9,1},{17,25},{25,17},{2,10},{10... | collective-permute-start | bytes 98312 | tf_op jit(solution)/shard_map/ppermute | solution.py:408
  9.8 9.2 %prepare.1 = (bf16[4,256,12288]{2,1,0:T(8,128)(2,1)S(1)}, f32[8,128]{1,0:T(8,128)S(1)}) custom-call(s32[2]{0:T(128)S(1)} %pad_add_fusion.ids_ref.e_ref.refs_0_, f32[4,48,128,256]{3,2,1,0:T(8,128)} %src.1), custom_call_target="tpu_custom_call" | custom-call | flops 25165824 | bytes 50331648 | tf_op jit(solution)/shard_map/prepare/pallas_call | solution.py:30
  19.6 2.6 %collective-permute-start.8 = (f32[16,512]{1,0:T(8,128)S(1)}, f32[16,512]{1,0:T(8,128)S(1)}, u32[]{:S(2)}, u32[]{:S(2)}) collective-permute-start(f32[16,512]{1,0:T(8,128)S(1)} %get-tuple-element.57), channel_id=1, source_target_pairs={{0,16},{8,24},{16,0},{24,8},{1,17},{9,25},{17,1},{25,9},{2,18},{10... | collective-permute-start | bytes 98312 | tf_op jit(solution)/shard_map/ppermute | solution.py:408
  25.0 3.6 %collective-permute-done.9.refs_3_ = f32[16,512]{1,0:T(8,128)S(1)} collective-permute-done((f32[16,512]{1,0:T(8,128)S(1)}, f32[16,512]{1,0:T(8,128)S(1)}, u32[]{:S(2)}, u32[]{:S(2)}) %collective-permute-start.9) | collective-permute-done | bytes 32800 | tf_op jit(solution)/shard_map/ppermute | solution.py:408
  29.3 12.4 %apply_first.1 = (f32[16,2048]{1,0:T(8,128)S(1)}, f32[16,2048]{1,0:T(8,128)S(1)}, f32[16,2048]{1,0:T(8,128)S(1)}, f32[16,2048]{1,0:T(8,128)S(1)}, f32[16,2048]{1...) custom-call(s32[2]{0:T(128)S(1)} %pad_add_fusion.ids_ref.e_ref.refs_0_, ...), custom_call_target="tpu_custom_call" | custom-call | flops 402653184 | bytes 25165824 | tf_op jit(solution)/shard_map/apply_first/pallas_call | solution.py:30
  43.1 2.5 %collective-permute-start.12 = (f32[16,2048]{1,0:T(8,128)S(1)}, f32[16,2048]{1,0:T(8,128)S(1)}, u32[]{:S(2)}, u32[]{:S(2)}) collective-permute-start(f32[16,2048]{1,0:T(8,128)S(1)} %add.48), channel_id=1, source_target_pairs={{0,6},{1,7},{2,4},{3,5},{4,2},{5,3},{6,0},{7,1},{8,14},{9,15},{10,... | collective-permute-start | bytes 393224 | tf_op jit(solution)/shard_map/ppermute | solution.py:408
  46.9 3.0 %collective-permute-done.12.refs_2_ = f32[16,2048]{1,0:T(8,128)S(1)} collective-permute-done((f32[16,2048]{1,0:T(8,128)S(1)}, f32[16,2048]{1,0:T(8,128)S(1)}, u32[]{:S(2)}, u32[]{:S(2)}) %collective-permute-start.12) | collective-permute-done | bytes 131104 | tf_op jit(solution)/shard_map/ppermute | solution.py:408
  49.8 2.6 %collective-permute-done.14.refs_3_ = f32[16,2048]{1,0:T(8,128)S(1)} collective-permute-done((f32[16,2048]{1,0:T(8,128)S(1)}, f32[16,2048]{1,0:T(8,128)S(1)}, u32[]{:S(2)}, u32[]{:S(2)}) %collective-permute-start.14) | collective-permute-done | bytes 131104 | tf_op jit(solution)/shard_map/ppermute | solution.py:408
  52.6 1.9 %collective-permute-start.22 = (f32[16,2176]{1,0:T(8,128)S(1)}, f32[16,2176]{1,0:T(8,128)S(1)}, u32[]{:S(2)}, u32[]{:S(2)}) collective-permute-start(f32[16,2176]{1,0:T(8,128)S(1)} %update_first.1.refs_2_.refs_6_), channel_id=1, source_target_pairs={{0,6},{1,7},{2,4},{3,5},{4,2},{5,3},{6,0},{7,1},{8,14},{9,15},{10,... | collective-permute-start | bytes 417800 | tf_op jit(solution)/shard_map/ppermute | solution.py:408
  56.2 4.0 %collective-permute-done.22.refs_8_ = f32[16,2176]{1,0:T(8,128)S(1)} collective-permute-done((f32[16,2176]{1,0:T(8,128)S(1)}, f32[16,2176]{1,0:T(8,128)S(1)}, u32[]{:S(2)}, u32[]{:S(2)}) %collective-permute-start.22) | collective-permute-done | bytes 139296 | tf_op jit(solution)/shard_map/ppermute | solution.py:408
  60.2 1.9 %collective-permute-done.20.refs_6_ = f32[16,2176]{1,0:T(8,128)S(1)} collective-permute-done((f32[16,2176]{1,0:T(8,128)S(1)}, f32[16,2176]{1,0:T(8,128)S(1)}, u32[]{:S(2)}, u32[]{:S(2)}) %collective-permute-start.20) | collective-permute-done | bytes 139296 | tf_op jit(solution)/shard_map/ppermute | solution.py:408
  63.6 11.1 %apply_zero.1 = (f32[16,2176]{1,0:T(8,128)S(1)}, f32[16,2176]{1,0:T(8,128)S(1)}, f32[16,2176]{1,0:T(8,128)S(1)}, f32[16,2176]{1,0:T(8,128)S(1)}, f32[16,2176]{1,...) custom-call(s32[2]{0:T(128)S(1)} %pad_add_fusion.ids_ref.e_ref.refs_, ...), custom_call_target="tpu_custom_call" | custom-call | flops 402653184 | bytes 25165824 | tf_op jit(solution)/shard_map/apply_zero/pallas_call | solution.py:30
  77.7 1.6 collective-permute-start.28
  80.0 3.8 %collective-permute-done.26.refs_2_ = f32[16,2176]{1,0:T(8,128)S(1)} collective-permute-done((f32[16,2176]{1,0:T(8,128)S(1)}, f32[16,2176]{1,0:T(8,128)S(1)}, u32[]{:S(2)}, u32[]{:S(2)}) %collective-permute-start.26) | collective-permute-done | bytes 139296 | tf_op jit(solution)/shard_map/ppermute | solution.py:408
  83.8 2.3 %collective-permute-done.28.refs_3_ = f32[16,2176]{1,0:T(8,128)S(1)} collective-permute-done((f32[16,2176]{1,0:T(8,128)S(1)}, f32[16,2176]{1,0:T(8,128)S(1)}, u32[]{:S(2)}, u32[]{:S(2)}) %collective-permute-start.28) | collective-permute-done | bytes 139296 | tf_op jit(solution)/shard_map/ppermute | solution.py:408
  86.4 1.5 collective-permute-start.36
  89.9 4.0 %collective-permute-done.36.refs_8_ = f32[16,2176]{1,0:T(8,128)S(1)} collective-permute-done((f32[16,2176]{1,0:T(8,128)S(1)}, f32[16,2176]{1,0:T(8,128)S(1)}, u32[]{:S(2)}, u32[]{:S(2)}) %collective-permute-start.36) | collective-permute-done | bytes 139296 | tf_op jit(solution)/shard_map/ppermute | solution.py:408
  93.9 1.9 %collective-permute-done.34.refs_6_ = f32[16,2176]{1,0:T(8,128)S(1)} collective-permute-done((f32[16,2176]{1,0:T(8,128)S(1)}, f32[16,2176]{1,0:T(8,128)S(1)}, u32[]{:S(2)}, u32[]{:S(2)}) %collective-permute-start.34) | collective-permute-done | bytes 139296 | tf_op jit(solution)/shard_map/ppermute | solution.py:408
  97.4 12.4 %apply_mid.1 = (f32[16,2176]{1,0:T(8,128)S(1)}, f32[16,2176]{1,0:T(8,128)S(1)}, f32[16,2176]{1,0:T(8,128)S(1)}, f32[16,2176]{1,0:T(8,128)S(1)}, f32[16,2176]{1,0...) custom-call(s32[2]{0:T(128)S(1)} %pad_add_fusion.ids_ref.e_ref.refs_, ...), custom_call_target="tpu_custom_call" | custom-call | flops 402653184 | bytes 25165824 | tf_op jit(solution)/shard_map/apply_mid/pallas_call | solution.py:30
  112.7 1.7 %collective-permute-start.42 = (f32[16,2176]{1,0:T(8,128)S(1)}, f32[16,2176]{1,0:T(8,128)S(1)}, u32[]{:S(2)}, u32[]{:S(2)}) collective-permute-start(f32[16,2176]{1,0:T(8,128)S(1)} %add.55), channel_id=1, source_target_pairs={{0,4},{1,5},{2,6},{3,7},{4,0},{5,1},{6,2},{7,3},{8,12},{9,13},{10,... | collective-permute-start | bytes 417800 | tf_op jit(solution)/shard_map/ppermute | solution.py:408
  115.0 3.8 %collective-permute-done.40.refs_2_ = f32[16,2176]{1,0:T(8,128)S(1)} collective-permute-done((f32[16,2176]{1,0:T(8,128)S(1)}, f32[16,2176]{1,0:T(8,128)S(1)}, u32[]{:S(2)}, u32[]{:S(2)}) %collective-permute-start.40) | collective-permute-done | bytes 139296 | tf_op jit(solution)/shard_map/ppermute | solution.py:408
  118.8 2.3 %collective-permute-done.42.refs_3_ = f32[16,2176]{1,0:T(8,128)S(1)} collective-permute-done((f32[16,2176]{1,0:T(8,128)S(1)}, f32[16,2176]{1,0:T(8,128)S(1)}, u32[]{:S(2)}, u32[]{:S(2)}) %collective-permute-start.42) | collective-permute-done | bytes 139296 | tf_op jit(solution)/shard_map/ppermute | solution.py:408
  121.4 1.5 collective-permute-start.50
  125.0 4.0 %collective-permute-done.50.refs_8_ = f32[16,2176]{1,0:T(8,128)S(1)} collective-permute-done((f32[16,2176]{1,0:T(8,128)S(1)}, f32[16,2176]{1,0:T(8,128)S(1)}, u32[]{:S(2)}, u32[]{:S(2)}) %collective-permute-start.50) | collective-permute-done | bytes 139296 | tf_op jit(solution)/shard_map/ppermute | solution.py:408
  129.0 1.9 %collective-permute-done.48.refs_6_ = f32[16,2176]{1,0:T(8,128)S(1)} collective-permute-done((f32[16,2176]{1,0:T(8,128)S(1)}, f32[16,2176]{1,0:T(8,128)S(1)}, u32[]{:S(2)}, u32[]{:S(2)}) %collective-permute-start.48) | collective-permute-done | bytes 139296 | tf_op jit(solution)/shard_map/ppermute | solution.py:408
  132.4 7.4 %apply_last.1 = (f32[16,128]{1,0:T(8,128)S(1)}, f32[16,2048]{1,0:T(8,128)S(1)}, f32[16,128]{1,0:T(8,128)S(1)}) custom-call(s32[2]{0:T(128)S(1)} %pad_add_fusion.ids_ref.e_ref.refs_0_, s32[4,48]{1,0:T(4,128)S(1)} %copy-done.5, f32[16,2176]{1,0:T(8,128)S(1)} %get-tuple-element.90.refs_2_, f32[16,2176]{1,0:T(8,128)S(1)} %collective-permute-done.45.refs_3_, ...), custom_call_target="tpu_custom_call" | custom-call | flops 402653184 | bytes 25165824 | tf_op jit(solution)/shard_map/apply_last/pallas_call | solution.py:30
  143.0 1.6 collective-permute-start.53
  144.7 1.5 collective-permute-done.54.refs_3_
  150.3 3.0 %collective-permute-start.58 = (f32[16,512]{1,0:T(8,128)S(1)}, f32[16,512]{1,0:T(8,128)S(1)}, u32[]{:S(2)}, u32[]{:S(2)}) collective-permute-start(f32[16,512]{1,0:T(8,128)S(1)} %get-tuple-element.100), channel_id=1, source_target_pairs={{0,24},{8,16},{16,8},{24,0},{1,25},{9,17},{17,9},{25,1},{2,26},{10... | collective-permute-start | bytes 98312 | tf_op jit(solution)/shard_map/ppermute | solution.py:408
  153.7 2.3 %collective-permute-done.58.refs_3_ = f32[16,512]{1,0:T(8,128)S(1)} collective-permute-done((f32[16,512]{1,0:T(8,128)S(1)}, f32[16,512]{1,0:T(8,128)S(1)}, u32[]{:S(2)}, u32[]{:S(2)}) %collective-permute-start.58) | collective-permute-done | bytes 32800 | tf_op jit(solution)/shard_map/ppermute | solution.py:408
  156.0 9.1 %shrink.1 = (f32[64,512]{1,0:T(8,128)}, f32[64,512]{1,0:T(8,128)}) custom-call(s32[2]{0:T(128)S(1)} %pad_add_fusion.ids_ref.e_ref.refs_0_, f32[16,512]{1,0:T(8,128)S(1)} %get-tuple-element.97.refs_0_, f32[16,512]{1,0:T(8,128)S(1)} %collective-permute-done.56.refs_1_, f32[16,512]{1,0:T(8,128)S(1)} %collective-permute-done.57.refs_2_, ...), custom_call_target="tpu_custom_call" | custom-call | tf_op jit(solution)/shard_map/shrink/pallas_call | solution.py:30
  (131 shorter events, 35.7 us)
Async XLA Ops:
  0.6 23.0 %collective-permute-start.5 = (f32[16,2048]{1,0:T(8,128)}, f32[16,2048]{1,0:T(8,128)S(1)}, u32[]{:S(2)}, u32[]{:S(2)}) collective-permute-start(f32[16,2048]{1,0:T(8,128)} %refs_5_.3), channel_id=1, source_target_pairs={{0,6},{1,7},{2,4},{3,5},{4,2},{5,3},{6,0},{7,1},{8,14},{9,15},{10,... | collective-permute-start | bytes 393224 | tf_op jit(solution)/shard_map/ppermute | solution.py:408
  4.6 15.0 %collective-permute-start.3 = (f32[16,2048]{1,0:T(8,128)}, f32[16,2048]{1,0:T(8,128)S(1)}, u32[]{:S(2)}, u32[]{:S(2)}) collective-permute-start(f32[16,2048]{1,0:T(8,128)} %refs_5_.3), channel_id=1, source_target_pairs={{0,4},{1,5},{2,6},{3,7},{4,0},{5,1},{6,2},{7,3},{8,12},{9,13},{10,... | collective-permute-start | bytes 393224 | tf_op jit(solution)/shard_map/ppermute | solution.py:408
  5.1 17.7 %collective-permute-start.1 = (f32[16,2048]{1,0:T(8,128)}, f32[16,2048]{1,0:T(8,128)S(1)}, u32[]{:S(2)}, u32[]{:S(2)}) collective-permute-start(f32[16,2048]{1,0:T(8,128)} %refs_5_.3), channel_id=1, source_target_pairs={{0,2},{1,3},{2,0},{3,1},{4,6},{5,7},{6,4},{7,5},{8,10},{9,11},{10,... | collective-permute-start | bytes 393224 | tf_op jit(solution)/shard_map/ppermute | solution.py:408
  5.3 23.9 %collective-permute-start = (f32[16,2048]{1,0:T(8,128)}, f32[16,2048]{1,0:T(8,128)S(1)}, u32[]{:S(2)}, u32[]{:S(2)}) collective-permute-start(f32[16,2048]{1,0:T(8,128)} %refs_5_.3), channel_id=1, source_target_pairs={{0,1},{1,0},{2,3},{3,2},{4,5},{5,4},{6,7},{7,6},{8,9},{9,8},{10,11... | collective-permute-start | bytes 393224 | tf_op jit(solution)/shard_map/ppermute | solution.py:408
  7.7 16.6 %collective-permute-start.7 = (f32[16,512]{1,0:T(8,128)S(1)}, f32[16,512]{1,0:T(8,128)S(1)}, u32[]{:S(2)}, u32[]{:S(2)}) collective-permute-start(f32[16,512]{1,0:T(8,128)S(1)} %get-tuple-element.56), channel_id=1, source_target_pairs={{0,8},{8,0},{16,24},{24,16},{1,9},{9,1},{17,25},{25,17},{2,10},{10... | collective-permute-start | bytes 98312 | tf_op jit(solution)/shard_map/ppermute | solution.py:408
  19.6 5.3 %collective-permute-start.8 = (f32[16,512]{1,0:T(8,128)S(1)}, f32[16,512]{1,0:T(8,128)S(1)}, u32[]{:S(2)}, u32[]{:S(2)}) collective-permute-start(f32[16,512]{1,0:T(8,128)S(1)} %get-tuple-element.57), channel_id=1, source_target_pairs={{0,16},{8,24},{16,0},{24,8},{1,17},{9,25},{17,1},{25,9},{2,18},{10... | collective-permute-start | bytes 98312 | tf_op jit(solution)/shard_map/ppermute | solution.py:408
  22.8 5.8 %collective-permute-start.9 = (f32[16,512]{1,0:T(8,128)S(1)}, f32[16,512]{1,0:T(8,128)S(1)}, u32[]{:S(2)}, u32[]{:S(2)}) collective-permute-start(f32[16,512]{1,0:T(8,128)S(1)} %get-tuple-element.58), channel_id=1, source_target_pairs={{0,24},{8,16},{16,8},{24,0},{1,25},{9,17},{17,9},{25,1},{2,26},{10... | collective-permute-start | bytes 98312 | tf_op jit(solution)/shard_map/ppermute | solution.py:408
  23.6 5.6 %collective-permute-start.2 = (f32[16,2048]{1,0:T(8,128)S(1)}, f32[16,2048]{1,0:T(8,128)S(1)}, u32[]{:S(2)}, u32[]{:S(2)}) collective-permute-start(f32[16,2048]{1,0:T(8,128)S(1)} %broadcast_add_fusion.2.refs_4_), channel_id=1, source_target_pairs={{0,1},{1,0},{2,3},{3,2},{4,5},{5,4},{6,7},{7,6},{8,9},{9,8},{10,11... | collective-permute-start | bytes 393224 | tf_op jit(solution)/shard_map/ppermute | solution.py:408
  24.4 4.9 %collective-permute-start.6 = (f32[16,2048]{1,0:T(8,128)S(1)}, f32[16,2048]{1,0:T(8,128)S(1)}, u32[]{:S(2)}, u32[]{:S(2)}) collective-permute-start(f32[16,2048]{1,0:T(8,128)S(1)} %broadcast_add_fusion.refs_8_), channel_id=1, source_target_pairs={{0,1},{1,0},{2,3},{3,2},{4,5},{5,4},{6,7},{7,6},{8,9},{9,8},{10,11... | collective-permute-start | bytes 393224 | tf_op jit(solution)/shard_map/ppermute | solution.py:408
  43.1 6.7 %collective-permute-start.12 = (f32[16,2048]{1,0:T(8,128)S(1)}, f32[16,2048]{1,0:T(8,128)S(1)}, u32[]{:S(2)}, u32[]{:S(2)}) collective-permute-start(f32[16,2048]{1,0:T(8,128)S(1)} %add.48), channel_id=1, source_target_pairs={{0,6},{1,7},{2,4},{3,5},{4,2},{5,3},{6,0},{7,1},{8,14},{9,15},{10,... | collective-permute-start | bytes 393224 | tf_op jit(solution)/shard_map/ppermute | solution.py:408
  45.7 6.8 %collective-permute-start.14 = (f32[16,2048]{1,0:T(8,128)S(1)}, f32[16,2048]{1,0:T(8,128)S(1)}, u32[]{:S(2)}, u32[]{:S(2)}) collective-permute-start(f32[16,2048]{1,0:T(8,128)S(1)} %add.49), channel_id=1, source_target_pairs={{0,4},{1,5},{2,6},{3,7},{4,0},{5,1},{6,2},{7,3},{8,12},{9,13},{10,... | collective-permute-start | bytes 393224 | tf_op jit(solution)/shard_map/ppermute | solution.py:408
  46.3 6.3 %collective-permute-start.16 = (f32[16,2048]{1,0:T(8,128)S(1)}, f32[16,2048]{1,0:T(8,128)S(1)}, u32[]{:S(2)}, u32[]{:S(2)}) collective-permute-start(f32[16,2048]{1,0:T(8,128)S(1)} %add.50), channel_id=1, source_target_pairs={{0,2},{1,3},{2,0},{3,1},{4,6},{5,7},{6,4},{7,5},{8,10},{9,11},{10,... | collective-permute-start | bytes 393224 | tf_op jit(solution)/shard_map/ppermute | solution.py:408
  52.6 7.5 %collective-permute-start.22 = (f32[16,2176]{1,0:T(8,128)S(1)}, f32[16,2176]{1,0:T(8,128)S(1)}, u32[]{:S(2)}, u32[]{:S(2)}) collective-permute-start(f32[16,2176]{1,0:T(8,128)S(1)} %update_first.1.refs_2_.refs_6_), channel_id=1, source_target_pairs={{0,6},{1,7},{2,4},{3,5},{4,2},{5,3},{6,0},{7,1},{8,14},{9,15},{10,... | collective-permute-start | bytes 417800 | tf_op jit(solution)/shard_map/ppermute | solution.py:408
  54.5 7.6 %collective-permute-start.20 = (f32[16,2176]{1,0:T(8,128)S(1)}, f32[16,2176]{1,0:T(8,128)S(1)}, u32[]{:S(2)}, u32[]{:S(2)}) collective-permute-start(f32[16,2176]{1,0:T(8,128)S(1)} %update_first.1.refs_2_.refs_6_), channel_id=1, source_target_pairs={{0,4},{1,5},{2,6},{3,7},{4,0},{5,1},{6,2},{7,3},{8,12},{9,13},{10,... | collective-permute-start | bytes 417800 | tf_op jit(solution)/shard_map/ppermute | solution.py:408
  55.7 6.5 %collective-permute-start.18 = (f32[16,2176]{1,0:T(8,128)S(1)}, f32[16,2176]{1,0:T(8,128)S(1)}, u32[]{:S(2)}, u32[]{:S(2)}) collective-permute-start(f32[16,2176]{1,0:T(8,128)S(1)} %update_first.1.refs_2_.refs_6_), channel_id=1, source_target_pairs={{0,2},{1,3},{2,0},{3,1},{4,6},{5,7},{6,4},{7,5},{8,10},{9,11},{10,... | collective-permute-start | bytes 417800 | tf_op jit(solution)/shard_map/ppermute | solution.py:408
  56.2 6.4 %collective-permute-start.17 = (f32[16,2176]{1,0:T(8,128)S(1)}, f32[16,2176]{1,0:T(8,128)S(1)}, u32[]{:S(2)}, u32[]{:S(2)}) collective-permute-start(f32[16,2176]{1,0:T(8,128)S(1)} %update_first.1.refs_2_.refs_6_), channel_id=1, source_target_pairs={{0,1},{1,0},{2,3},{3,2},{4,5},{5,4},{6,7},{7,6},{8,9},{9,8},{10,11... | collective-permute-start | bytes 417800 | tf_op jit(solution)/shard_map/ppermute | solution.py:408
  76.2 7.6 %collective-permute-start.26 = (f32[16,2176]{1,0:T(8,128)S(1)}, f32[16,2176]{1,0:T(8,128)S(1)}, u32[]{:S(2)}, u32[]{:S(2)}) collective-permute-start(f32[16,2176]{1,0:T(8,128)S(1)} %add.51), channel_id=1, source_target_pairs={{0,6},{1,7},{2,4},{3,5},{4,2},{5,3},{6,0},{7,1},{8,14},{9,15},{10,... | collective-permute-start | bytes 417800 | tf_op jit(solution)/shard_map/ppermute | solution.py:408
  77.7 8.4 %collective-permute-start.28 = (f32[16,2176]{1,0:T(8,128)S(1)}, f32[16,2176]{1,0:T(8,128)S(1)}, u32[]{:S(2)}, u32[]{:S(2)}) collective-permute-start(f32[16,2176]{1,0:T(8,128)S(1)} %add.52), channel_id=1, source_target_pairs={{0,4},{1,5},{2,6},{3,7},{4,0},{5,1},{6,2},{7,3},{8,12},{9,13},{10,... | collective-permute-start | bytes 417800 | tf_op jit(solution)/shard_map/ppermute | solution.py:408
  79.4 6.8 %collective-permute-start.30 = (f32[16,2176]{1,0:T(8,128)S(1)}, f32[16,2176]{1,0:T(8,128)S(1)}, u32[]{:S(2)}, u32[]{:S(2)}) collective-permute-start(f32[16,2176]{1,0:T(8,128)S(1)} %add.53), channel_id=1, source_target_pairs={{0,2},{1,3},{2,0},{3,1},{4,6},{5,7},{6,4},{7,5},{8,10},{9,11},{10,... | collective-permute-start | bytes 417800 | tf_op jit(solution)/shard_map/ppermute | solution.py:408
  86.4 7.5 %collective-permute-start.36 = (f32[16,2176]{1,0:T(8,128)S(1)}, f32[16,2176]{1,0:T(8,128)S(1)}, u32[]{:S(2)}, u32[]{:S(2)}) collective-permute-start(f32[16,2176]{1,0:T(8,128)S(1)} %get-tuple-element.77.refs_2_.refs_6_), channel_id=1, source_target_pairs={{0,6},{1,7},{2,4},{3,5},{4,2},{5,3},{6,0},{7,1},{8,14},{9,15},{10,... | collective-permute-start | bytes 417800 | tf_op jit(solution)/shard_map/ppermute | solution.py:408
  87.9 7.9 %collective-permute-start.34 = (f32[16,2176]{1,0:T(8,128)S(1)}, f32[16,2176]{1,0:T(8,128)S(1)}, u32[]{:S(2)}, u32[]{:S(2)}) collective-permute-start(f32[16,2176]{1,0:T(8,128)S(1)} %get-tuple-element.77.refs_2_.refs_6_), channel_id=1, source_target_pairs={{0,4},{1,5},{2,6},{3,7},{4,0},{5,1},{6,2},{7,3},{8,12},{9,13},{10,... | collective-permute-start | bytes 417800 | tf_op jit(solution)/shard_map/ppermute | solution.py:408
  89.3 6.6 %collective-permute-start.32 = (f32[16,2176]{1,0:T(8,128)S(1)}, f32[16,2176]{1,0:T(8,128)S(1)}, u32[]{:S(2)}, u32[]{:S(2)}) collective-permute-start(f32[16,2176]{1,0:T(8,128)S(1)} %get-tuple-element.77.refs_2_.refs_6_), channel_id=1, source_target_pairs={{0,2},{1,3},{2,0},{3,1},{4,6},{5,7},{6,4},{7,5},{8,10},{9,11},{10,... | collective-permute-start | bytes 417800 | tf_op jit(solution)/shard_map/ppermute | solution.py:408
  89.9 6.4 %collective-permute-start.31 = (f32[16,2176]{1,0:T(8,128)S(1)}, f32[16,2176]{1,0:T(8,128)S(1)}, u32[]{:S(2)}, u32[]{:S(2)}) collective-permute-start(f32[16,2176]{1,0:T(8,128)S(1)} %get-tuple-element.77.refs_2_.refs_6_), channel_id=1, source_target_pairs={{0,1},{1,0},{2,3},{3,2},{4,5},{5,4},{6,7},{7,6},{8,9},{9,8},{10,11... | collective-permute-start | bytes 417800 | tf_op jit(solution)/shard_map/ppermute | solution.py:408
  111.3 7.6 %collective-permute-start.40 = (f32[16,2176]{1,0:T(8,128)S(1)}, f32[16,2176]{1,0:T(8,128)S(1)}, u32[]{:S(2)}, u32[]{:S(2)}) collective-permute-start(f32[16,2176]{1,0:T(8,128)S(1)} %add.54), channel_id=1, source_target_pairs={{0,6},{1,7},{2,4},{3,5},{4,2},{5,3},{6,0},{7,1},{8,14},{9,15},{10,... | collective-permute-start | bytes 417800 | tf_op jit(solution)/shard_map/ppermute | solution.py:408
  112.7 8.4 %collective-permute-start.42 = (f32[16,2176]{1,0:T(8,128)S(1)}, f32[16,2176]{1,0:T(8,128)S(1)}, u32[]{:S(2)}, u32[]{:S(2)}) collective-permute-start(f32[16,2176]{1,0:T(8,128)S(1)} %add.55), channel_id=1, source_target_pairs={{0,4},{1,5},{2,6},{3,7},{4,0},{5,1},{6,2},{7,3},{8,12},{9,13},{10,... | collective-permute-start | bytes 417800 | tf_op jit(solution)/shard_map/ppermute | solution.py:408
  114.4 6.8 %collective-permute-start.44 = (f32[16,2176]{1,0:T(8,128)S(1)}, f32[16,2176]{1,0:T(8,128)S(1)}, u32[]{:S(2)}, u32[]{:S(2)}) collective-permute-start(f32[16,2176]{1,0:T(8,128)S(1)} %add.56), channel_id=1, source_target_pairs={{0,2},{1,3},{2,0},{3,1},{4,6},{5,7},{6,4},{7,5},{8,10},{9,11},{10,... | collective-permute-start | bytes 417800 | tf_op jit(solution)/shard_map/ppermute | solution.py:408
  121.4 7.5 %collective-permute-start.50 = (f32[16,2176]{1,0:T(8,128)S(1)}, f32[16,2176]{1,0:T(8,128)S(1)}, u32[]{:S(2)}, u32[]{:S(2)}) collective-permute-start(f32[16,2176]{1,0:T(8,128)S(1)} %get-tuple-element.90.refs_2_), channel_id=1, source_target_pairs={{0,6},{1,7},{2,4},{3,5},{4,2},{5,3},{6,0},{7,1},{8,14},{9,15},{10,... | collective-permute-start | bytes 417800 | tf_op jit(solution)/shard_map/ppermute | solution.py:408
  122.9 8.0 %collective-permute-start.48 = (f32[16,2176]{1,0:T(8,128)S(1)}, f32[16,2176]{1,0:T(8,128)S(1)}, u32[]{:S(2)}, u32[]{:S(2)}) collective-permute-start(f32[16,2176]{1,0:T(8,128)S(1)} %get-tuple-element.90.refs_2_), channel_id=1, source_target_pairs={{0,4},{1,5},{2,6},{3,7},{4,0},{5,1},{6,2},{7,3},{8,12},{9,13},{10,... | collective-permute-start | bytes 417800 | tf_op jit(solution)/shard_map/ppermute | solution.py:408
  124.4 6.6 %collective-permute-start.46 = (f32[16,2176]{1,0:T(8,128)S(1)}, f32[16,2176]{1,0:T(8,128)S(1)}, u32[]{:S(2)}, u32[]{:S(2)}) collective-permute-start(f32[16,2176]{1,0:T(8,128)S(1)} %get-tuple-element.90.refs_2_), channel_id=1, source_target_pairs={{0,2},{1,3},{2,0},{3,1},{4,6},{5,7},{6,4},{7,5},{8,10},{9,11},{10,... | collective-permute-start | bytes 417800 | tf_op jit(solution)/shard_map/ppermute | solution.py:408
  125.0 6.4 %collective-permute-start.45 = (f32[16,2176]{1,0:T(8,128)S(1)}, f32[16,2176]{1,0:T(8,128)S(1)}, u32[]{:S(2)}, u32[]{:S(2)}) collective-permute-start(f32[16,2176]{1,0:T(8,128)S(1)} %get-tuple-element.90.refs_2_), channel_id=1, source_target_pairs={{0,1},{1,0},{2,3},{3,2},{4,5},{5,4},{6,7},{7,6},{8,9},{9,8},{10,11... | collective-permute-start | bytes 417800 | tf_op jit(solution)/shard_map/ppermute | solution.py:408
  148.9 4.8 %collective-permute-start.57 = (f32[16,512]{1,0:T(8,128)S(1)}, f32[16,512]{1,0:T(8,128)S(1)}, u32[]{:S(2)}, u32[]{:S(2)}) collective-permute-start(f32[16,512]{1,0:T(8,128)S(1)} %get-tuple-element.99), channel_id=1, source_target_pairs={{0,16},{8,24},{16,0},{24,8},{1,17},{9,25},{17,1},{25,9},{2,18},{10... | collective-permute-start | bytes 98312 | tf_op jit(solution)/shard_map/ppermute | solution.py:408
  150.3 5.7 %collective-permute-start.58 = (f32[16,512]{1,0:T(8,128)S(1)}, f32[16,512]{1,0:T(8,128)S(1)}, u32[]{:S(2)}, u32[]{:S(2)}) collective-permute-start(f32[16,512]{1,0:T(8,128)S(1)} %get-tuple-element.100), channel_id=1, source_target_pairs={{0,24},{8,16},{16,8},{24,0},{1,25},{9,17},{17,9},{25,1},{2,26},{10... | collective-permute-start | bytes 98312 | tf_op jit(solution)/shard_map/ppermute | solution.py:408
  (35 other events, 239.2 us)
where the time goes:
time: 165 us
  Pallas kernels  64.7 us (39%)
  waiting for transfers between devices  50.3 us (30%)
  starting transfers between devices  44.6 us (27%)
  local copies, waits for them, and re-layouts  2.34 us (1%)
  other arithmetic  2.28 us (1%)
    pallas_call x12, Pallas kernels, call(): pl.pallas_call(body, out_shape=outs, in_specs=specs, out_specs=out_specs...  64.7 us
    ppermute x59, waiting for transfers between devices, swap(): return lax.ppermute(x, axis, [(i, i ^ k) for i in range(size)])  50.3 us
    ppermute x59, starting transfers between devices, swap(): return lax.ppermute(x, axis, [(i, i ^ k) for i in range(size)])  44.6 us
  transfers between devices with their start and end apart: 59, of which 34 were waited for; matrix products, arithmetic and copies ran while one was open for 2% of the time, Pallas kernels for 6%

commit v1 on v0

--- a/solution.py
+++ b/solution.py
@@ -1,11 +1,10 @@
-import functools
-
 import jax
 import jax.numpy as jnp
 from jax import lax
 from jax.experimental import pallas as pl
 from jax.experimental.pallas import tpu as pltpu
 from jax.sharding import PartitionSpec as P
+
 
 PV = 64
 ITERS = 3
@@ -26,7 +25,7 @@
     return jax.ShapeDtypeStruct(shape, dtype)
 
 
-def call(body, outs, ins, specs, scratch=(), limit=12, flops=0, moved=0, out_specs=None, name=None):
+def call(body, outs, ins, specs, scratch=(), limit=12, flops=0, moved=0, out_specs=None):
     return pl.pallas_call(
         body,
         out_shape=outs,
@@ -35,7 +34,6 @@
         scratch_shapes=list(scratch),
         compiler_params=pltpu.CompilerParams(vmem_limit_bytes=limit * MIB),
         cost_estimate=pl.CostEstimate(flops=flops, bytes_accessed=moved, transcendentals=0),
-        name=name,
     )(*ins)
 
 
@@ -49,9 +47,7 @@
     per = T // step
     trips = R * per
 
-    def body(ids_ref, src, out, token, buf, sem):
-        token[...] = jnp.zeros_like(token)
-
+    def body(ids_ref, src, out, buf, sem):
         def copy(i):
             slot = lax.rem(i, depth)
             at = lax.rem(i, per) * step
@@ -79,13 +75,12 @@
 
     return call(
         body,
-        [pltpu.VMEM((R, 2 * rays, T * width), BF16), sds((8, LANES))],
+        pltpu.VMEM((R, 2 * rays, T * width), BF16),
         (ids, tiles),
         [SM, ANY],
         [pltpu.VMEM((depth, step, rays, width), F32), pltpu.SemaphoreType.DMA((depth,))],
         moved=tiles.size * 8,
         flops=tiles.size * 4,
-        name="prepare",
     )
 
 
@@ -98,7 +93,7 @@
     pieces = [next(it) for _ in range(n)]
     tt, scale_ref = next(it), next(it)
     if mode == "first":
-        sino, _ = next(it), next(it)
+        sino = next(it)
     if mode in ("mid", "last"):
         d_prev, ad_prev, rr_prev = next(it), next(it), next(it)
     if mode != "last":
@@ -169,6 +164,7 @@
         return
 
     acc[...] = jnp.zeros_like(acc)
+
     def back(r, carry):
         lhs = weighted[r]
 
@@ -222,7 +218,6 @@
         scratch,
         flops=4 * C * R * T * rays * vb,
         moved=R * T * rays * vb * 4,
-        name="apply_" + mode,
     )
 
 
@@ -246,7 +241,7 @@
         out[:, :seg] = r
         out[:, seg:] = fold(r * r)
 
-    return call(body, sds((C, seg + LANES)), (*parts, volume, target), [VM] * (len(parts) + 2), name="update_first")
+    return call(body, sds((C, seg + LANES)), (*parts, volume, target), [VM] * (len(parts) + 2))
 
 
 def update(parts, volume, residual, direction, rr):
@@ -270,7 +265,6 @@
         [sds((C, seg)), sds((C, seg + LANES))],
         (*parts, volume, residual, direction, rr),
         [VM] * (len(parts) + 4),
-        name="update",
     )
 
 
@@ -296,7 +290,6 @@
         [sds((C, seg))] + [sds((C, width))] * E,
         (group, *parts, volume, direction, rr),
         [SM] + [VM] * (len(parts) + 3),
-        name="finish",
     )
     return got[0], got[1:]
 
@@ -310,7 +303,7 @@
             at = pl.multiple_of((e_ref[1] ^ k) * C, 8)
             outs[k][...] = st[pl.ds(at, C), :] - sd[pl.ds(at, C), :]
 
-    return call(body, [sds((C, width))] * E, (group, split_target, scaled_dual), [SM, VM, VM], name="target_pieces")
+    return call(body, [sds((C, width))] * E, (group, split_target, scaled_dual), [SM, VM, VM])
 
 
 def join_target(pieces, group):
@@ -322,7 +315,7 @@
             at = pl.multiple_of((e_ref[1] ^ k) * width, LANES)
             refs[E][:, pl.ds(at, width)] = refs[k][...]
 
-    return call(body, sds((C, width * E)), (group, *pieces), [SM] + [VM] * E, name="join_target")
+    return call(body, sds((C, width * E)), (group, *pieces), [SM] + [VM] * E)
 
 
 def shrink(pieces, scaled_dual, group):
@@ -400,7 +393,6 @@
             pltpu.VMEM((N, patches, 2 * PV), F32),
             pltpu.VMEM((patches * N, 2 * PV), F32),
         ],
-        name="shrink",
     )
 
 
@@ -408,13 +400,11 @@
     return lax.ppermute(x, axis, [(i, i ^ k) for i in range(size)])
 
 
-def gather(own, n, between=None):
+def gather(own, n):
     pieces = [None] * n
     pieces[0] = own
     for j in range(n // 2 - 1, 0, -1):
         pieces[2 * j] = swap(own, "views", n, 2 * j)
-    if between is not None:
-        pieces[2::2] = [piece + between for piece in pieces[2::2]]
     for j in range(n // 2):
         pieces[2 * j + 1] = swap(pieces[2 * j], "views", n, 1)
     return pieces
@@ -426,7 +416,8 @@
         got[j] = swap(send[j], "views", n, 1)
     parts = [keep[0], got[0]]
     for j in range(n // 2 - 1, 0, -1):
-        parts.append(swap(keep[j] + got[j], "views", n, 2 * j))
+        total = keep[j] + got[j]
+        parts.append(swap(total, "views", n, 2 * j))
     return parts
 
 
@@ -440,13 +431,14 @@
     scale = ray_weights * live.reshape(1, -1)
     split_target, scaled_dual = split_target[0], scaled_dual[0]
 
-    tt, token = prepare(tiles, me, 8)
-    tp = split_target_pieces(split_target, scaled_dual, group, E)
-    pieces = gather(start, n, token[0, 0])
-    tp = [tp[0]] + [swap(tp[k], "energy", E, k) for k in range(1, E)]
+    tt = prepare(tiles, me, 8)
+    tp = list(split_target_pieces(split_target, scaled_dual, group, E))
+    pieces = gather(start, n)
+    for k in range(1, E):
+        tp[k] = swap(tp[k], "energy", E, k)
     target = join_target(tp, group)
 
-    out = apply("first", dims, me, tile_blocks, *pieces, tt, scale, sinogram, target)
+    out = apply("first", dims, me, tile_blocks, *pieces, tt, scale, sinogram)
     parts = scatter_sum(out[: n // 2], out[n // 2 : n], n)
     residual = update_first(parts, start, target)
     volume = start

time: 165 us -> 165 us (level)
  starting transfers between devices: 44.6 us -> 49 us
  local copies, waits for them, and re-layouts: 2.34 us -> 0.03 us
  other arithmetic: 2.28 us -> 0.31 us
    ppermute x59, starting transfers between devices: 44.6 us -> 49 us  [swap(): return lax.ppermute(x, axis, [(i, i ^ k) for i in range(size)])]
    add x12 -> x9, other arithmetic: 2.12 us -> 0.15 us  [scatter_sum(): total = keep[j] + got[j]]
    unnamed x16 -> x14, local copies, waits for them, and re-layouts: 1.83 us -> 0.03 us
  transfers between devices with their start and end apart: 59 -> 59, of which waited for: 34 -> 36; matrix products, arithmetic and copies ran while one was open for 2% -> 0% of each run, Pallas kernels for 6% -> 6%
where the time goes in v1:
time: 165 us
  Pallas kernels  64.7 us (39%)
  waiting for transfers between devices  50.1 us (30%)
  starting transfers between devices  49 us (30%)
    pallas_call x12, Pallas kernels, call(): pl.pallas_call(body, out_shape=outs, in_specs=specs, out_specs=out_specs...  64.7 us
    ppermute x59, waiting for transfers between devices, swap(): return lax.ppermute(x, axis, [(i, i ^ k) for i in range(size)])  50.1 us
    ppermute x59, starting transfers between devices, swap(): return lax.ppermute(x, axis, [(i, i ^ k) for i in range(size)])  49 us
  transfers between devices with their start and end apart: 59, of which 36 were waited for; matrix products, arithmetic and copies ran while one was open for 0% of the time, Pallas kernels for 6%

profile of v1, /device:TPU:0, one launch (start us, length us, event | category | flops | bytes accessed | tf_op | source)
XLA Modules:
  0.0 165.0 jit_solution(1591916156389399575)
XLA Ops:
  0.6 4.0 %collective-permute-start.5 = (f32[16,2048]{1,0:T(8,128)}, f32[16,2048]{1,0:T(8,128)S(1)}, u32[]{:S(2)}, u32[]{:S(2)}) collective-permute-start(f32[16,2048]{1,0:T(8,128)} %refs_5_.3), channel_id=1, source_target_pairs={{0,6},{1,7},{2,4},{3,5},{4,2},{5,3},{6,0},{7,1},{8,14},{9,15},{10,... | collective-permute-start | bytes 393224 | tf_op jit(solution)/shard_map/ppermute | solution.py:400
  5.4 9.2 %shard_map.103.refs_10_ = bf16[4,256,12288]{2,1,0:T(8,128)(2,1)S(1)} custom-call(s32[2]{0:T(128)S(1)} %pad_add_fusion.ids_ref.refs_0_.e_ref, f32[4,48,128,256]{3,2,1,0:T(8,128)} %src.1), custom_call_target="tpu_custom_call" | custom-call | flops 25165824 | bytes 50331648 | tf_op jit(solution)/shard_map/pallas_call | solution.py:29
  16.8 12.4 %shard_map.104 = (f32[16,2048]{1,0:T(8,128)S(1)}, f32[16,2048]{1,0:T(8,128)S(1)}, f32[16,2048]{1,0:T(8,128)S(1)}, f32[16,2048]{1,0:T(8,128)S(1)}, f32[16,2048]{1...) custom-call(s32[2]{0:T(128)S(1)} %pad_add_fusion.ids_ref.refs_0_.e_ref, ...), custom_call_target="tpu_custom_call" | custom-call | flops 402653184 | bytes 25165824 | tf_op jit(solution)/shard_map/pallas_call | solution.py:29
  30.6 2.9 %collective-permute-start.9 = (f32[16,2048]{1,0:T(8,128)S(1)}, f32[16,2048]{1,0:T(8,128)S(1)}, u32[]{:S(2)}, u32[]{:S(2)}) collective-permute-start(f32[16,2048]{1,0:T(8,128)S(1)} %add.30), channel_id=1, source_target_pairs={{0,6},{1,7},{2,4},{3,5},{4,2},{5,3},{6,0},{7,1},{8,14},{9,15},{10,... | collective-permute-start | bytes 393224 | tf_op jit(solution)/shard_map/ppermute | solution.py:400
  35.1 1.9 %collective-permute-start.14 = (f32[16,512]{1,0:T(8,128)S(1)}, f32[16,512]{1,0:T(8,128)S(1)}, u32[]{:S(2)}, u32[]{:S(2)}) collective-permute-start(f32[16,512]{1,0:T(8,128)S(1)} %get-tuple-element.60), channel_id=1, source_target_pairs={{0,8},{8,0},{16,24},{24,16},{1,9},{9,1},{17,25},{25,17},{2,10},{10... | collective-permute-start | bytes 98312 | tf_op jit(solution)/shard_map/ppermute | solution.py:400
  37.0 2.1 %collective-permute-done.14.refs_1_ = f32[16,512]{1,0:T(8,128)S(1)} collective-permute-done((f32[16,512]{1,0:T(8,128)S(1)}, f32[16,512]{1,0:T(8,128)S(1)}, u32[]{:S(2)}, u32[]{:S(2)}) %collective-permute-start.14) | collective-permute-done | bytes 32800 | tf_op jit(solution)/shard_map/ppermute | solution.py:400
  39.1 2.8 %collective-permute-start.15 = (f32[16,512]{1,0:T(8,128)S(1)}, f32[16,512]{1,0:T(8,128)S(1)}, u32[]{:S(2)}, u32[]{:S(2)}) collective-permute-start(f32[16,512]{1,0:T(8,128)S(1)} %get-tuple-element.61), channel_id=1, source_target_pairs={{0,16},{8,24},{16,0},{24,8},{1,17},{9,25},{17,1},{25,9},{2,18},{10... | collective-permute-start | bytes 98312 | tf_op jit(solution)/shard_map/ppermute | solution.py:400
  41.9 2.0 %collective-permute-done.15.refs_2_ = f32[16,512]{1,0:T(8,128)S(1)} collective-permute-done((f32[16,512]{1,0:T(8,128)S(1)}, f32[16,512]{1,0:T(8,128)S(1)}, u32[]{:S(2)}, u32[]{:S(2)}) %collective-permute-start.15) | collective-permute-done | bytes 32800 | tf_op jit(solution)/shard_map/ppermute | solution.py:400
  43.9 4.3 %collective-permute-start.16 = (f32[16,512]{1,0:T(8,128)S(1)}, f32[16,512]{1,0:T(8,128)S(1)}, u32[]{:S(2)}, u32[]{:S(2)}) collective-permute-start(f32[16,512]{1,0:T(8,128)S(1)} %get-tuple-element.62), channel_id=1, source_target_pairs={{0,24},{8,16},{16,8},{24,0},{1,25},{9,17},{17,9},{25,1},{2,26},{10... | collective-permute-start | bytes 98312 | tf_op jit(solution)/shard_map/ppermute | solution.py:400
  48.2 1.9 %collective-permute-done.16.refs_3_ = f32[16,512]{1,0:T(8,128)S(1)} collective-permute-done((f32[16,512]{1,0:T(8,128)S(1)}, f32[16,512]{1,0:T(8,128)S(1)}, u32[]{:S(2)}, u32[]{:S(2)}) %collective-permute-start.16) | collective-permute-done | bytes 32800 | tf_op jit(solution)/shard_map/ppermute | solution.py:400
  50.8 2.5 %collective-permute-start.22 = (f32[16,2176]{1,0:T(8,128)S(1)}, f32[16,2176]{1,0:T(8,128)S(1)}, u32[]{:S(2)}, u32[]{:S(2)}) collective-permute-start(f32[16,2176]{1,0:T(8,128)S(1)} %shard_map.107.refs_2_.refs_6_), channel_id=1, source_target_pairs={{0,6},{1,7},{2,4},{3,5},{4,2},{5,3},{6,0},{7,1},{8,14},{9,15},{10,... | collective-permute-start | bytes 417800 | tf_op jit(solution)/shard_map/ppermute | solution.py:400
  54.4 2.5 %collective-permute-done.22.refs_8_ = f32[16,2176]{1,0:T(8,128)S(1)} collective-permute-done((f32[16,2176]{1,0:T(8,128)S(1)}, f32[16,2176]{1,0:T(8,128)S(1)}, u32[]{:S(2)}, u32[]{:S(2)}) %collective-permute-start.22) | collective-permute-done | bytes 139296 | tf_op jit(solution)/shard_map/ppermute | solution.py:400
  60.2 11.1 %shard_map.108 = (f32[16,2176]{1,0:T(8,128)S(1)}, f32[16,2176]{1,0:T(8,128)S(1)}, f32[16,2176]{1,0:T(8,128)S(1)}, f32[16,2176]{1,0:T(8,128)S(1)}, f32[16,2176]{1...) custom-call(s32[2]{0:T(128)S(1)} %pad_add_fusion.ids_ref.refs_0_.e_r, ...), custom_call_target="tpu_custom_call" | custom-call | flops 402653184 | bytes 25165824 | tf_op jit(solution)/shard_map/pallas_call | solution.py:29
  72.8 1.7 %collective-permute-start.26 = (f32[16,2176]{1,0:T(8,128)S(1)}, f32[16,2176]{1,0:T(8,128)S(1)}, u32[]{:S(2)}, u32[]{:S(2)}) collective-permute-start(f32[16,2176]{1,0:T(8,128)S(1)} %add.33), channel_id=1, source_target_pairs={{0,6},{1,7},{2,4},{3,5},{4,2},{5,3},{6,0},{7,1},{8,14},{9,15},{10,... | collective-permute-start | bytes 417800 | tf_op jit(solution)/shard_map/ppermute | solution.py:400
  76.5 3.8 %collective-permute-done.26.refs_2_ = f32[16,2176]{1,0:T(8,128)S(1)} collective-permute-done((f32[16,2176]{1,0:T(8,128)S(1)}, f32[16,2176]{1,0:T(8,128)S(1)}, u32[]{:S(2)}, u32[]{:S(2)}) %collective-permute-start.26) | collective-permute-done | bytes 139296 | tf_op jit(solution)/shard_map/ppermute | solution.py:400
  80.3 2.2 %collective-permute-done.28.refs_3_ = f32[16,2176]{1,0:T(8,128)S(1)} collective-permute-done((f32[16,2176]{1,0:T(8,128)S(1)}, f32[16,2176]{1,0:T(8,128)S(1)}, u32[]{:S(2)}, u32[]{:S(2)}) %collective-permute-start.28) | collective-permute-done | bytes 139296 | tf_op jit(solution)/shard_map/ppermute | solution.py:400
  82.8 1.8 %collective-permute-start.36 = (f32[16,2176]{1,0:T(8,128)S(1)}, f32[16,2176]{1,0:T(8,128)S(1)}, u32[]{:S(2)}, u32[]{:S(2)}) collective-permute-start(f32[16,2176]{1,0:T(8,128)S(1)} %get-tuple-element.73.refs_2_.refs_6_), channel_id=1, source_target_pairs={{0,6},{1,7},{2,4},{3,5},{4,2},{5,3},{6,0},{7,1},{8,14},{9,15},{10,... | collective-permute-start | bytes 417800 | tf_op jit(solution)/shard_map/ppermute | solution.py:400
  86.4 4.0 %collective-permute-done.36.refs_8_ = f32[16,2176]{1,0:T(8,128)S(1)} collective-permute-done((f32[16,2176]{1,0:T(8,128)S(1)}, f32[16,2176]{1,0:T(8,128)S(1)}, u32[]{:S(2)}, u32[]{:S(2)}) %collective-permute-start.36) | collective-permute-done | bytes 139296 | tf_op jit(solution)/shard_map/ppermute | solution.py:400
  90.3 1.9 %collective-permute-done.34.refs_6_ = f32[16,2176]{1,0:T(8,128)S(1)} collective-permute-done((f32[16,2176]{1,0:T(8,128)S(1)}, f32[16,2176]{1,0:T(8,128)S(1)}, u32[]{:S(2)}, u32[]{:S(2)}) %collective-permute-start.34) | collective-permute-done | bytes 139296 | tf_op jit(solution)/shard_map/ppermute | solution.py:400
  93.8 12.4 %shard_map.110 = (f32[16,2176]{1,0:T(8,128)S(1)}, f32[16,2176]{1,0:T(8,128)S(1)}, f32[16,2176]{1,0:T(8,128)S(1)}, f32[16,2176]{1,0:T(8,128)S(1)}, f32[16,2176]{1...) custom-call(s32[2]{0:T(128)S(1)} %pad_add_fusion.ids_ref.refs_0_.e_r, ...), custom_call_target="tpu_custom_call" | custom-call | flops 402653184 | bytes 25165824 | tf_op jit(solution)/shard_map/pallas_call | solution.py:29
  107.7 1.8 %collective-permute-start.40 = (f32[16,2176]{1,0:T(8,128)S(1)}, f32[16,2176]{1,0:T(8,128)S(1)}, u32[]{:S(2)}, u32[]{:S(2)}) collective-permute-start(f32[16,2176]{1,0:T(8,128)S(1)} %add.36), channel_id=1, source_target_pairs={{0,6},{1,7},{2,4},{3,5},{4,2},{5,3},{6,0},{7,1},{8,14},{9,15},{10,... | collective-permute-start | bytes 417800 | tf_op jit(solution)/shard_map/ppermute | solution.py:400
  111.4 3.8 %collective-permute-done.40.refs_2_ = f32[16,2176]{1,0:T(8,128)S(1)} collective-permute-done((f32[16,2176]{1,0:T(8,128)S(1)}, f32[16,2176]{1,0:T(8,128)S(1)}, u32[]{:S(2)}, u32[]{:S(2)}) %collective-permute-start.40) | collective-permute-done | bytes 139296 | tf_op jit(solution)/shard_map/ppermute | solution.py:400
  115.2 2.3 %collective-permute-done.42.refs_3_ = f32[16,2176]{1,0:T(8,128)S(1)} collective-permute-done((f32[16,2176]{1,0:T(8,128)S(1)}, f32[16,2176]{1,0:T(8,128)S(1)}, u32[]{:S(2)}, u32[]{:S(2)}) %collective-permute-start.42) | collective-permute-done | bytes 139296 | tf_op jit(solution)/shard_map/ppermute | solution.py:400
  117.9 1.7 %collective-permute-start.50 = (f32[16,2176]{1,0:T(8,128)S(1)}, f32[16,2176]{1,0:T(8,128)S(1)}, u32[]{:S(2)}, u32[]{:S(2)}) collective-permute-start(f32[16,2176]{1,0:T(8,128)S(1)} %get-tuple-element.86.refs_2_), channel_id=1, source_target_pairs={{0,6},{1,7},{2,4},{3,5},{4,2},{5,3},{6,0},{7,1},{8,14},{9,15},{10,... | collective-permute-start | bytes 417800 | tf_op jit(solution)/shard_map/ppermute | solution.py:400
  121.4 3.9 %collective-permute-done.50.refs_8_ = f32[16,2176]{1,0:T(8,128)S(1)} collective-permute-done((f32[16,2176]{1,0:T(8,128)S(1)}, f32[16,2176]{1,0:T(8,128)S(1)}, u32[]{:S(2)}, u32[]{:S(2)}) %collective-permute-start.50) | collective-permute-done | bytes 139296 | tf_op jit(solution)/shard_map/ppermute | solution.py:400
  125.4 1.9 %collective-permute-done.48.refs_6_ = f32[16,2176]{1,0:T(8,128)S(1)} collective-permute-done((f32[16,2176]{1,0:T(8,128)S(1)}, f32[16,2176]{1,0:T(8,128)S(1)}, u32[]{:S(2)}, u32[]{:S(2)}) %collective-permute-start.48) | collective-permute-done | bytes 139296 | tf_op jit(solution)/shard_map/ppermute | solution.py:400
  128.9 7.4 %shard_map.112 = (f32[16,128]{1,0:T(8,128)S(1)}, f32[16,2048]{1,0:T(8,128)S(1)}, f32[16,128]{1,0:T(8,128)S(1)}) custom-call(s32[2]{0:T(128)S(1)} %pad_add_fusion.ids_ref.refs_0_.e_ref, s32[4,48]{1,0:T(4,128)S(1)} %copy-done.4, f32[16,2176]{1,0:T(8,128)S(1)} %get-tuple-element.86.refs_2_, f32[16,2176]{1,0:T(8,128)S(1)} %collective-permute-done.45.refs_3_, ...), custom_call_target="tpu_custom_call" | custom-call | flops 402653184 | bytes 25165824 | tf_op jit(solution)/shard_map/pallas_call | solution.py:29
  142.4 1.9 %collective-permute-done.53.refs_2_ = f32[16,128]{1,0:T(8,128)S(1)} collective-permute-done((f32[16,128]{1,0:T(8,128)S(1)}, f32[16,128]{1,0:T(8,128)S(1)}, u32[]{:S(2)}, u32[]{:S(2)}) %collective-permute-start.53) | collective-permute-done | bytes 8224 | tf_op jit(solution)/shard_map/ppermute | solution.py:400
  145.7 4.4 %collective-permute-start.57 = (f32[16,512]{1,0:T(8,128)S(1)}, f32[16,512]{1,0:T(8,128)S(1)}, u32[]{:S(2)}, u32[]{:S(2)}) collective-permute-start(f32[16,512]{1,0:T(8,128)S(1)} %get-tuple-element.95), channel_id=1, source_target_pairs={{0,16},{8,24},{16,0},{24,8},{1,17},{9,25},{17,1},{25,9},{2,18},{10... | collective-permute-start | bytes 98312 | tf_op jit(solution)/shard_map/ppermute | solution.py:400
  150.1 2.2 %collective-permute-done.57.refs_2_ = f32[16,512]{1,0:T(8,128)S(1)} collective-permute-done((f32[16,512]{1,0:T(8,128)S(1)}, f32[16,512]{1,0:T(8,128)S(1)}, u32[]{:S(2)}, u32[]{:S(2)}) %collective-permute-start.57) | collective-permute-done | bytes 32800 | tf_op jit(solution)/shard_map/ppermute | solution.py:400
  152.4 3.5 %collective-permute-done.58.refs_3_ = f32[16,512]{1,0:T(8,128)S(1)} collective-permute-done((f32[16,512]{1,0:T(8,128)S(1)}, f32[16,512]{1,0:T(8,128)S(1)}, u32[]{:S(2)}, u32[]{:S(2)}) %collective-permute-start.58) | collective-permute-done | bytes 32800 | tf_op jit(solution)/shard_map/ppermute | solution.py:400
  155.8 9.1 %shard_map.114 = (f32[64,512]{1,0:T(8,128)}, f32[64,512]{1,0:T(8,128)}) custom-call(s32[2]{0:T(128)S(1)} %pad_add_fusion.ids_ref.refs_0_.e_ref, f32[16,512]{1,0:T(8,128)S(1)} %get-tuple-element.93.refs_0_, f32[16,512]{1,0:T(8,128)S(1)} %collective-permute-done.56.refs_1_, f32[16,512]{1,0:T(8,128)S(1)} %collective-permute-done.57.refs_2_, ...), custom_call_target="tpu_custom_call" | custom-call | tf_op jit(solution)/shard_map/pallas_call | solution.py:29
  (125 shorter events, 32.6 us)
Async XLA Ops:
  0.6 14.1 %collective-permute-start.5 = (f32[16,2048]{1,0:T(8,128)}, f32[16,2048]{1,0:T(8,128)S(1)}, u32[]{:S(2)}, u32[]{:S(2)}) collective-permute-start(f32[16,2048]{1,0:T(8,128)} %refs_5_.3), channel_id=1, source_target_pairs={{0,6},{1,7},{2,4},{3,5},{4,2},{5,3},{6,0},{7,1},{8,14},{9,15},{10,... | collective-permute-start | bytes 393224 | tf_op jit(solution)/shard_map/ppermute | solution.py:400
  4.6 10.6 %collective-permute-start.3 = (f32[16,2048]{1,0:T(8,128)}, f32[16,2048]{1,0:T(8,128)S(1)}, u32[]{:S(2)}, u32[]{:S(2)}) collective-permute-start(f32[16,2048]{1,0:T(8,128)} %refs_5_.3), channel_id=1, source_target_pairs={{0,4},{1,5},{2,6},{3,7},{4,0},{5,1},{6,2},{7,3},{8,12},{9,13},{10,... | collective-permute-start | bytes 393224 | tf_op jit(solution)/shard_map/ppermute | solution.py:400
  5.1 10.2 %collective-permute-start.1 = (f32[16,2048]{1,0:T(8,128)}, f32[16,2048]{1,0:T(8,128)S(1)}, u32[]{:S(2)}, u32[]{:S(2)}) collective-permute-start(f32[16,2048]{1,0:T(8,128)} %refs_5_.3), channel_id=1, source_target_pairs={{0,2},{1,3},{2,0},{3,1},{4,6},{5,7},{6,4},{7,5},{8,10},{9,11},{10,... | collective-permute-start | bytes 393224 | tf_op jit(solution)/shard_map/ppermute | solution.py:400
  5.3 10.5 %collective-permute-start = (f32[16,2048]{1,0:T(8,128)}, f32[16,2048]{1,0:T(8,128)S(1)}, u32[]{:S(2)}, u32[]{:S(2)}) collective-permute-start(f32[16,2048]{1,0:T(8,128)} %refs_5_.3), channel_id=1, source_target_pairs={{0,1},{1,0},{2,3},{3,2},{4,5},{5,4},{6,7},{7,6},{8,9},{9,8},{10,11... | collective-permute-start | bytes 393224 | tf_op jit(solution)/shard_map/ppermute | solution.py:400
  30.1 20.6 %collective-permute-start.7 = (f32[16,2048]{1,0:T(8,128)S(1)}, f32[16,2048]{1,0:T(8,128)S(1)}, u32[]{:S(2)}, u32[]{:S(2)}) collective-permute-start(f32[16,2048]{1,0:T(8,128)S(1)} %get-tuple-element.52), channel_id=1, source_target_pairs={{0,1},{1,0},{2,3},{3,2},{4,5},{5,4},{6,7},{7,6},{8,9},{9,8},{10,11... | collective-permute-start | bytes 393224 | tf_op jit(solution)/shard_map/ppermute | solution.py:400
  30.6 20.1 %collective-permute-start.9 = (f32[16,2048]{1,0:T(8,128)S(1)}, f32[16,2048]{1,0:T(8,128)S(1)}, u32[]{:S(2)}, u32[]{:S(2)}) collective-permute-start(f32[16,2048]{1,0:T(8,128)S(1)} %add.30), channel_id=1, source_target_pairs={{0,6},{1,7},{2,4},{3,5},{4,2},{5,3},{6,0},{7,1},{8,14},{9,15},{10,... | collective-permute-start | bytes 393224 | tf_op jit(solution)/shard_map/ppermute | solution.py:400
  33.6 17.1 %collective-permute-start.11 = (f32[16,2048]{1,0:T(8,128)S(1)}, f32[16,2048]{1,0:T(8,128)S(1)}, u32[]{:S(2)}, u32[]{:S(2)}) collective-permute-start(f32[16,2048]{1,0:T(8,128)S(1)} %add.31), channel_id=1, source_target_pairs={{0,4},{1,5},{2,6},{3,7},{4,0},{5,1},{6,2},{7,3},{8,12},{9,13},{10,... | collective-permute-start | bytes 393224 | tf_op jit(solution)/shard_map/ppermute | solution.py:400
  34.2 16.5 %collective-permute-start.13 = (f32[16,2048]{1,0:T(8,128)S(1)}, f32[16,2048]{1,0:T(8,128)S(1)}, u32[]{:S(2)}, u32[]{:S(2)}) collective-permute-start(f32[16,2048]{1,0:T(8,128)S(1)} %add.32), channel_id=1, source_target_pairs={{0,2},{1,3},{2,0},{3,1},{4,6},{5,7},{6,4},{7,5},{8,10},{9,11},{10,... | collective-permute-start | bytes 393224 | tf_op jit(solution)/shard_map/ppermute | solution.py:400
  39.1 4.8 %collective-permute-start.15 = (f32[16,512]{1,0:T(8,128)S(1)}, f32[16,512]{1,0:T(8,128)S(1)}, u32[]{:S(2)}, u32[]{:S(2)}) collective-permute-start(f32[16,512]{1,0:T(8,128)S(1)} %get-tuple-element.61), channel_id=1, source_target_pairs={{0,16},{8,24},{16,0},{24,8},{1,17},{9,25},{17,1},{25,9},{2,18},{10... | collective-permute-start | bytes 98312 | tf_op jit(solution)/shard_map/ppermute | solution.py:400
  43.9 6.2 %collective-permute-start.16 = (f32[16,512]{1,0:T(8,128)S(1)}, f32[16,512]{1,0:T(8,128)S(1)}, u32[]{:S(2)}, u32[]{:S(2)}) collective-permute-start(f32[16,512]{1,0:T(8,128)S(1)} %get-tuple-element.62), channel_id=1, source_target_pairs={{0,24},{8,16},{16,8},{24,0},{1,25},{9,17},{17,9},{25,1},{2,26},{10... | collective-permute-start | bytes 98312 | tf_op jit(solution)/shard_map/ppermute | solution.py:400
  50.8 6.0 %collective-permute-start.22 = (f32[16,2176]{1,0:T(8,128)S(1)}, f32[16,2176]{1,0:T(8,128)S(1)}, u32[]{:S(2)}, u32[]{:S(2)}) collective-permute-start(f32[16,2176]{1,0:T(8,128)S(1)} %shard_map.107.refs_2_.refs_6_), channel_id=1, source_target_pairs={{0,6},{1,7},{2,4},{3,5},{4,2},{5,3},{6,0},{7,1},{8,14},{9,15},{10,... | collective-permute-start | bytes 417800 | tf_op jit(solution)/shard_map/ppermute | solution.py:400
  53.3 5.1 %collective-permute-start.20 = (f32[16,2176]{1,0:T(8,128)S(1)}, f32[16,2176]{1,0:T(8,128)S(1)}, u32[]{:S(2)}, u32[]{:S(2)}) collective-permute-start(f32[16,2176]{1,0:T(8,128)S(1)} %shard_map.107.refs_2_.refs_6_), channel_id=1, source_target_pairs={{0,4},{1,5},{2,6},{3,7},{4,0},{5,1},{6,2},{7,3},{8,12},{9,13},{10,... | collective-permute-start | bytes 417800 | tf_op jit(solution)/shard_map/ppermute | solution.py:400
  53.8 5.1 %collective-permute-start.18 = (f32[16,2176]{1,0:T(8,128)S(1)}, f32[16,2176]{1,0:T(8,128)S(1)}, u32[]{:S(2)}, u32[]{:S(2)}) collective-permute-start(f32[16,2176]{1,0:T(8,128)S(1)} %shard_map.107.refs_2_.refs_6_), channel_id=1, source_target_pairs={{0,2},{1,3},{2,0},{3,1},{4,6},{5,7},{6,4},{7,5},{8,10},{9,11},{10,... | collective-permute-start | bytes 417800 | tf_op jit(solution)/shard_map/ppermute | solution.py:400
  54.4 4.5 %collective-permute-start.17 = (f32[16,2176]{1,0:T(8,128)S(1)}, f32[16,2176]{1,0:T(8,128)S(1)}, u32[]{:S(2)}, u32[]{:S(2)}) collective-permute-start(f32[16,2176]{1,0:T(8,128)S(1)} %shard_map.107.refs_2_.refs_6_), channel_id=1, source_target_pairs={{0,1},{1,0},{2,3},{3,2},{4,5},{5,4},{6,7},{7,6},{8,9},{9,8},{10,11... | collective-permute-start | bytes 417800 | tf_op jit(solution)/shard_map/ppermute | solution.py:400
  72.1 4.5 %collective-permute-start.24 = (f32[16,2176]{1,0:T(8,128)S(1)}, f32[16,2176]{1,0:T(8,128)S(1)}, u32[]{:S(2)}, u32[]{:S(2)}) collective-permute-start(f32[16,2176]{1,0:T(8,128)S(1)} %get-tuple-element.64), channel_id=1, source_target_pairs={{0,1},{1,0},{2,3},{3,2},{4,5},{5,4},{6,7},{7,6},{8,9},{9,8},{10,11... | collective-permute-start | bytes 417800 | tf_op jit(solution)/shard_map/ppermute | solution.py:400
  72.8 7.5 %collective-permute-start.26 = (f32[16,2176]{1,0:T(8,128)S(1)}, f32[16,2176]{1,0:T(8,128)S(1)}, u32[]{:S(2)}, u32[]{:S(2)}) collective-permute-start(f32[16,2176]{1,0:T(8,128)S(1)} %add.33), channel_id=1, source_target_pairs={{0,6},{1,7},{2,4},{3,5},{4,2},{5,3},{6,0},{7,1},{8,14},{9,15},{10,... | collective-permute-start | bytes 417800 | tf_op jit(solution)/shard_map/ppermute | solution.py:400
  74.6 7.9 %collective-permute-start.28 = (f32[16,2176]{1,0:T(8,128)S(1)}, f32[16,2176]{1,0:T(8,128)S(1)}, u32[]{:S(2)}, u32[]{:S(2)}) collective-permute-start(f32[16,2176]{1,0:T(8,128)S(1)} %add.34), channel_id=1, source_target_pairs={{0,4},{1,5},{2,6},{3,7},{4,0},{5,1},{6,2},{7,3},{8,12},{9,13},{10,... | collective-permute-start | bytes 417800 | tf_op jit(solution)/shard_map/ppermute | solution.py:400
  75.6 7.0 %collective-permute-start.30 = (f32[16,2176]{1,0:T(8,128)S(1)}, f32[16,2176]{1,0:T(8,128)S(1)}, u32[]{:S(2)}, u32[]{:S(2)}) collective-permute-start(f32[16,2176]{1,0:T(8,128)S(1)} %add.35), channel_id=1, source_target_pairs={{0,2},{1,3},{2,0},{3,1},{4,6},{5,7},{6,4},{7,5},{8,10},{9,11},{10,... | collective-permute-start | bytes 417800 | tf_op jit(solution)/shard_map/ppermute | solution.py:400
  82.8 7.5 %collective-permute-start.36 = (f32[16,2176]{1,0:T(8,128)S(1)}, f32[16,2176]{1,0:T(8,128)S(1)}, u32[]{:S(2)}, u32[]{:S(2)}) collective-permute-start(f32[16,2176]{1,0:T(8,128)S(1)} %get-tuple-element.73.refs_2_.refs_6_), channel_id=1, source_target_pairs={{0,6},{1,7},{2,4},{3,5},{4,2},{5,3},{6,0},{7,1},{8,14},{9,15},{10,... | collective-permute-start | bytes 417800 | tf_op jit(solution)/shard_map/ppermute | solution.py:400
  84.6 7.7 %collective-permute-start.34 = (f32[16,2176]{1,0:T(8,128)S(1)}, f32[16,2176]{1,0:T(8,128)S(1)}, u32[]{:S(2)}, u32[]{:S(2)}) collective-permute-start(f32[16,2176]{1,0:T(8,128)S(1)} %get-tuple-element.73.refs_2_.refs_6_), channel_id=1, source_target_pairs={{0,4},{1,5},{2,6},{3,7},{4,0},{5,1},{6,2},{7,3},{8,12},{9,13},{10,... | collective-permute-start | bytes 417800 | tf_op jit(solution)/shard_map/ppermute | solution.py:400
  85.5 6.8 %collective-permute-start.32 = (f32[16,2176]{1,0:T(8,128)S(1)}, f32[16,2176]{1,0:T(8,128)S(1)}, u32[]{:S(2)}, u32[]{:S(2)}) collective-permute-start(f32[16,2176]{1,0:T(8,128)S(1)} %get-tuple-element.73.refs_2_.refs_6_), channel_id=1, source_target_pairs={{0,2},{1,3},{2,0},{3,1},{4,6},{5,7},{6,4},{7,5},{8,10},{9,11},{10,... | collective-permute-start | bytes 417800 | tf_op jit(solution)/shard_map/ppermute | solution.py:400
  86.4 6.4 %collective-permute-start.31 = (f32[16,2176]{1,0:T(8,128)S(1)}, f32[16,2176]{1,0:T(8,128)S(1)}, u32[]{:S(2)}, u32[]{:S(2)}) collective-permute-start(f32[16,2176]{1,0:T(8,128)S(1)} %get-tuple-element.73.refs_2_.refs_6_), channel_id=1, source_target_pairs={{0,1},{1,0},{2,3},{3,2},{4,5},{5,4},{6,7},{7,6},{8,9},{9,8},{10,11... | collective-permute-start | bytes 417800 | tf_op jit(solution)/shard_map/ppermute | solution.py:400
  107.7 7.5 %collective-permute-start.40 = (f32[16,2176]{1,0:T(8,128)S(1)}, f32[16,2176]{1,0:T(8,128)S(1)}, u32[]{:S(2)}, u32[]{:S(2)}) collective-permute-start(f32[16,2176]{1,0:T(8,128)S(1)} %add.36), channel_id=1, source_target_pairs={{0,6},{1,7},{2,4},{3,5},{4,2},{5,3},{6,0},{7,1},{8,14},{9,15},{10,... | collective-permute-start | bytes 417800 | tf_op jit(solution)/shard_map/ppermute | solution.py:400
  109.5 8.0 %collective-permute-start.42 = (f32[16,2176]{1,0:T(8,128)S(1)}, f32[16,2176]{1,0:T(8,128)S(1)}, u32[]{:S(2)}, u32[]{:S(2)}) collective-permute-start(f32[16,2176]{1,0:T(8,128)S(1)} %add.37), channel_id=1, source_target_pairs={{0,4},{1,5},{2,6},{3,7},{4,0},{5,1},{6,2},{7,3},{8,12},{9,13},{10,... | collective-permute-start | bytes 417800 | tf_op jit(solution)/shard_map/ppermute | solution.py:400
  110.6 7.0 %collective-permute-start.44 = (f32[16,2176]{1,0:T(8,128)S(1)}, f32[16,2176]{1,0:T(8,128)S(1)}, u32[]{:S(2)}, u32[]{:S(2)}) collective-permute-start(f32[16,2176]{1,0:T(8,128)S(1)} %add.38), channel_id=1, source_target_pairs={{0,2},{1,3},{2,0},{3,1},{4,6},{5,7},{6,4},{7,5},{8,10},{9,11},{10,... | collective-permute-start | bytes 417800 | tf_op jit(solution)/shard_map/ppermute | solution.py:400
  117.9 7.5 %collective-permute-start.50 = (f32[16,2176]{1,0:T(8,128)S(1)}, f32[16,2176]{1,0:T(8,128)S(1)}, u32[]{:S(2)}, u32[]{:S(2)}) collective-permute-start(f32[16,2176]{1,0:T(8,128)S(1)} %get-tuple-element.86.refs_2_), channel_id=1, source_target_pairs={{0,6},{1,7},{2,4},{3,5},{4,2},{5,3},{6,0},{7,1},{8,14},{9,15},{10,... | collective-permute-start | bytes 417800 | tf_op jit(solution)/shard_map/ppermute | solution.py:400
  119.6 7.7 %collective-permute-start.48 = (f32[16,2176]{1,0:T(8,128)S(1)}, f32[16,2176]{1,0:T(8,128)S(1)}, u32[]{:S(2)}, u32[]{:S(2)}) collective-permute-start(f32[16,2176]{1,0:T(8,128)S(1)} %get-tuple-element.86.refs_2_), channel_id=1, source_target_pairs={{0,4},{1,5},{2,6},{3,7},{4,0},{5,1},{6,2},{7,3},{8,12},{9,13},{10,... | collective-permute-start | bytes 417800 | tf_op jit(solution)/shard_map/ppermute | solution.py:400
  120.6 6.8 %collective-permute-start.46 = (f32[16,2176]{1,0:T(8,128)S(1)}, f32[16,2176]{1,0:T(8,128)S(1)}, u32[]{:S(2)}, u32[]{:S(2)}) collective-permute-start(f32[16,2176]{1,0:T(8,128)S(1)} %get-tuple-element.86.refs_2_), channel_id=1, source_target_pairs={{0,2},{1,3},{2,0},{3,1},{4,6},{5,7},{6,4},{7,5},{8,10},{9,11},{10,... | collective-permute-start | bytes 417800 | tf_op jit(solution)/shard_map/ppermute | solution.py:400
  121.4 6.4 %collective-permute-start.45 = (f32[16,2176]{1,0:T(8,128)S(1)}, f32[16,2176]{1,0:T(8,128)S(1)}, u32[]{:S(2)}, u32[]{:S(2)}) collective-permute-start(f32[16,2176]{1,0:T(8,128)S(1)} %get-tuple-element.86.refs_2_), channel_id=1, source_target_pairs={{0,1},{1,0},{2,3},{3,2},{4,5},{5,4},{6,7},{7,6},{8,9},{9,8},{10,11... | collective-permute-start | bytes 417800 | tf_op jit(solution)/shard_map/ppermute | solution.py:400
  139.8 4.5 %collective-permute-start.53 = (f32[16,128]{1,0:T(8,128)S(1)}, f32[16,128]{1,0:T(8,128)S(1)}, u32[]{:S(2)}, u32[]{:S(2)}) collective-permute-start(f32[16,128]{1,0:T(8,128)S(1)} %add.39.refs_1_), channel_id=1, source_target_pairs={{0,6},{1,7},{2,4},{3,5},{4,2},{5,3},{6,0},{7,1},{8,14},{9,15},{10,... | collective-permute-start | bytes 24584 | tf_op jit(solution)/shard_map/ppermute | solution.py:400
  145.7 6.6 %collective-permute-start.57 = (f32[16,512]{1,0:T(8,128)S(1)}, f32[16,512]{1,0:T(8,128)S(1)}, u32[]{:S(2)}, u32[]{:S(2)}) collective-permute-start(f32[16,512]{1,0:T(8,128)S(1)} %get-tuple-element.95), channel_id=1, source_target_pairs={{0,16},{8,24},{16,0},{24,8},{1,17},{9,25},{17,1},{25,9},{2,18},{10... | collective-permute-start | bytes 98312 | tf_op jit(solution)/shard_map/ppermute | solution.py:400
  150.1 5.7 %collective-permute-start.58 = (f32[16,512]{1,0:T(8,128)S(1)}, f32[16,512]{1,0:T(8,128)S(1)}, u32[]{:S(2)}, u32[]{:S(2)}) collective-permute-start(f32[16,512]{1,0:T(8,128)S(1)} %get-tuple-element.96), channel_id=1, source_target_pairs={{0,24},{8,16},{16,8},{24,0},{1,25},{9,17},{17,9},{25,1},{2,26},{10... | collective-permute-start | bytes 98312 | tf_op jit(solution)/shard_map/ppermute | solution.py:400
  (34 other events, 160.3 us)
